TPU v7x, 32 devices: a whole 2x2x4 slice. The times are simulated.
32 devices in a mesh: grp: 2 (over y), dp: 16 (over z, x, core).
Axes of the slice: x: 2, y: 2, z: 4, core: 2. Of those that a mesh axis runs over, the one named last changes fastest.
Arguments:
- query_act: bfloat16 [32768, 256], P(('grp', 'dp')), parts along dimension 0, may hold values from -6 to 6
- query_grad: bfloat16 [32768, 256], P(('grp', 'dp')), parts along dimension 0, may hold values from -6 to 6
- train_act: bfloat16 [32, 64, 256], P(('grp', 'dp')), parts along dimension 0, may hold values from -12 to 12
- train_grad: bfloat16 [32, 64, 256], P(('grp', 'dp')), parts along dimension 0, may hold values from -12 to 12
- seq_ids: int32 [32, 64], P(('grp', 'dp')), parts along dimension 0, may hold values from 0 to 3, never falling along the last dimension, each value on 1 to 32 neighbouring positions
Outputs:
- scores: float32 [32768, 64], P(('grp', 'dp')), parts along dimension 0
There are 2 independent parts, one for each index of `grp`. A program takes and returns all parts, laid end to end along the dimension named above; each array names one. Nothing has to cross between parts.
Inputs may be any that keep to these rules, and one draw needn't show every extreme that they name: `seq_ids`: within a span the ids never fall and each of the 4 sequences holds 1 to 32 tokens, one exactly 32.
All inputs are finite; a program needn't handle non-finite values.
Results may differ from a plain program's by a relative error of at most 0.023.
The roundings to bfloat16 on the way count: a program that leaves them out, or rounds other values in their place, can miss the bound.
Values may be sent and summed in bfloat16 or wider, within the bound.
No kernel may reach another device: no remote copies, remote signals or barrier semaphores. Data moves between devices by JAX's collectives and lax.ppermute only.
A program may use at most 192 MiB of HBM per device.

v0:
```python
import math

import jax
import jax.numpy as jnp
from jax import lax
from jax.experimental import pallas as pl
from jax.experimental.pallas import tpu as pltpu
from jax.sharding import PartitionSpec as P

SEQ_DEV = 4
DAMPING = 0.1

BF16 = jnp.bfloat16
F32 = jnp.float32


FAST_STEPS = 7


def newton_schedule():
    radius, bounds, scales = 0.02, [], []
    for _ in range(13):
        before = math.sqrt(2.0 * radius / (1.0 + radius))
        scales.append(2.0 / (2.0 - before * before))
        bounds.append(2.0 * DAMPING / (1.0 - before) - DAMPING)
        radius = before
    return bounds, scales


BOUNDS, SCALES = newton_schedule()


def pick(steps, values):
    out = jnp.float32(values[FAST_STEPS - 1])
    for position in range(FAST_STEPS + 1, len(values) + 1):
        out = jnp.where(steps == position, jnp.float32(values[position - 1]), out)
    return out


def split2(x):
    high = x.astype(BF16)
    return high, (x - high.astype(F32)).astype(BF16)


def split3(x):
    high = x.astype(BF16)
    rest = x - high.astype(F32)
    mid = rest.astype(BF16)
    return high, mid, (rest - mid.astype(F32)).astype(BF16)


def dot(a, b):
    return jnp.dot(a, b, preferred_element_type=F32)


def dot3(a, b):
    return dot(a[0], b[0]) + (dot(a[0], b[1]) + dot(a[1], b[0]))


def dot6(a, b):
    small = dot(a[1], b[1]) + (dot(a[0], b[2]) + dot(a[2], b[0]))
    return dot(a[0], b[0]) + ((dot(a[0], b[1]) + dot(a[1], b[0])) + small)


def dot_nt(a, b):
    return lax.dot_general(a, b, (((1,), (1,)), ((), ())), preferred_element_type=F32)


def corrected(matrices, xs, eye):
    xparts = [split3(x) for x in xs]
    residuals = [eye - dot6(split3(matrix), parts) for matrix, parts in zip(matrices, xparts)]
    highs = [residual.astype(BF16) for residual in residuals]
    sums = [split2(residual + dot(high, high)) for residual, high in zip(residuals, highs)]
    return [x + dot3(parts, total) for x, parts, total in zip(xs, xparts, sums)]


def influence_kernel(rows, scale, *refs):
    n_pieces = len(refs) - 13
    pieces = refs[:n_pieces]
    query_act_hbm, query_grad_hbm, out, query_act, query_grad, act, grad, onehot, mat, tmat, xmat, inverse, arrived = refs[n_pieces:]
    loads = [
        pltpu.make_async_copy(query_act_hbm, query_act, arrived.at[0]),
        pltpu.make_async_copy(query_grad_hbm, query_grad, arrived.at[1]),
    ]
    for load in loads:
        load.start()
    tokens, width = act.shape
    columns = onehot.shape[0]
    lane = lax.broadcasted_iota(jnp.int32, (1, 128), 1)
    column = lax.broadcasted_iota(jnp.int32, (columns, 128), 0)

    spans = [(ref, k) for ref in pieces for k in range(ref.shape[0])]
    labels = []
    for slot, (ref, k) in enumerate(spans):
        act[slot * rows : (slot + 1) * rows, :] = ref[k, 0:rows, :]
        grad[slot * rows : (slot + 1) * rows, :] = ref[k, rows : 2 * rows, :]
        tail = ref[k, 2 * rows : 2 * rows + 8, 0:128].astype(F32)
        labels.append((SEQ_DEV * tail[1:2, :] + tail[0:1, :]).astype(jnp.int32))
    for pair in range(tokens // 128):
        label = jnp.where(lane < rows, labels[2 * pair], labels[2 * pair + 1])
        onehot[:, pair * 128 : (pair + 1) * 128] = (column == label).astype(F32).astype(BF16)

    diagonal = lax.broadcasted_iota(jnp.int32, (width, width), 0) == lax.broadcasted_iota(jnp.int32, (width, width), 1)
    eye = diagonal.astype(F32)
    covars = [
        lax.dot_general(flat, flat, (((0,), (0,)), ((), ())), preferred_element_type=F32) for flat in (act[...], grad[...])
    ]
    matrices = [covar * (1.0 / tokens) + DAMPING * eye for covar in covars]
    squares = [dot3(parts, parts) for parts in map(split2, matrices)]
    norm = jnp.maximum(jnp.sum(squares[0] * squares[0]), jnp.sum(squares[1] * squares[1]))

    steps = jnp.int32(FAST_STEPS)
    for bound in BOUNDS[FAST_STEPS - 1 : -1]:
        steps = steps + (norm > 0.99 * bound**4).astype(jnp.int32)

    def first_step(which, square, start, factor):
        t = start * matrices[which]
        return (factor * start) * (2.0 * eye - t), factor * (2.0 * t - (start * start) * square)

    start = 2.0 / (DAMPING + BOUNDS[FAST_STEPS - 1])
    both = [first_step(which, squares[which], start, SCALES[FAST_STEPS - 1]) for which in range(2)]
    for left in range(FAST_STEPS - 1, 0, -1):
        factor = SCALES[left - 1]
        tparts = [split2(t) for _, t in both]
        after = [t for _, t in both]
        if left > 1:
            after = [factor * (2.0 * t - dot3(parts, parts)) for (_, t), parts in zip(both, tparts)]
        both = [
            (factor * (2.0 * x - dot3(split2(x), parts)), t) for (x, _), parts, t in zip(both, tparts, after)
        ]
    for which in range(2):
        xmat[which] = both[which][0]

    @pl.when(steps > FAST_STEPS)
    def _():
        start = pick(steps, [2.0 / (DAMPING + bound) for bound in BOUNDS])
        factor = pick(steps, SCALES)
        for which in range(2):
            parts = split3(matrices[which])
            mat[which] = matrices[which]
            xmat[which], tmat[which] = first_step(which, dot6(parts, parts), start, factor)

        def step(i, carry):
            left = steps - i
            factor = jnp.float32(SCALES[0])
            for position in range(2, len(SCALES) + 1):
                factor = jnp.where(left == position, jnp.float32(SCALES[position - 1]), factor)
            for which in range(2):
                t, x = tmat[which], xmat[which]
                tparts, xparts = split3(t), split3(x)
                xmat[which] = factor * (2.0 * x - dot6(xparts, tparts))
                tmat[which] = factor * (2.0 * t - dot6(tparts, tparts))
            return carry

        lax.fori_loop(1, steps, step, 0)

        for which, x in enumerate(corrected([mat[0], mat[1]], [xmat[0], xmat[1]], eye)):
            xmat[which] = x

    for which, x in enumerate(corrected(matrices, [xmat[0], xmat[1]], eye)):
        inverse[2 * which], inverse[2 * which + 1] = split2(x)

    for load in loads:
        load.wait()
    block, chunk = min(1024, query_act.shape[0]), min(1024, tokens)

    def scores(i, carry):
        here = pl.ds(pl.multiple_of(i * block, block), block)
        qa, qg = query_act[here, :], query_grad[here, :]
        pa = (dot(qa, inverse[0]) + dot(qa, inverse[1])).astype(BF16)
        pg = (dot(qg, inverse[2]) + dot(qg, inverse[3])).astype(BF16)
        total = jnp.zeros((columns, block), F32)
        for first_token in range(0, tokens, chunk):
            these = slice(first_token, first_token + chunk)
            product = dot_nt(act[these, :], pa) * dot_nt(grad[these, :], pg)
            total = total + dot(onehot[:, these], product.astype(BF16))
        out[:, here] = total * scale
        return carry

    lax.fori_loop(0, query_act.shape[0] // block, scores, 0, unroll=tokens <= 1024)


def payload_kernel(rows, act, grad, ids, out):
    out[0, 0:rows, :] = act[0]
    out[0, rows : 2 * rows, :] = grad[0]
    index = lax.axis_index("dp").astype(F32)
    label = ids[...].astype(F32)
    label = jnp.broadcast_to(jnp.concatenate([label] * (act.shape[2] // rows), axis=1), (8, act.shape[2]))
    row = lax.broadcasted_iota(jnp.int32, label.shape, 0)
    out[0, 2 * rows :, :] = jnp.where(row == 0, label, index).astype(BF16)


ROUTE_16 = (
    ((0, 2), (0, 4), (0, 8), (3, 4), (3, 2), (2, 2), (3, 6))
    + ((7, 1), (6, 1), (5, 1), (4, 1), (1, 1), (2, 1), (3, 1), (0, 1))
)


def exchange(piece, bits, size):
    return lax.ppermute(piece, "dp", [(device, device ^ bits) for device in range(size)])


def gather_spans(payload, size):
    held = [payload]
    if size == 16:
        for source, bits in ROUTE_16:
            held.append(exchange(held[source], bits, size))
        return held
    for bit in reversed([1 << k for k in range(size.bit_length() - 1)]):
        if len(held) >= 16:
            held = [jnp.concatenate(held, axis=0)]
        held = held + [exchange(piece, bit, size) for piece in held]
    return held


def score_call(pieces, query_act, query_grad, rows):
    spans, queries, width = sum(piece.shape[0] for piece in pieces), query_act.shape[0], query_act.shape[1]
    tokens, columns = spans * rows, spans * SEQ_DEV
    vmem = pl.BlockSpec(memory_space=pltpu.VMEM)
    scale = 1.0 / (8.0 * math.sqrt(query_act.shape[1] * query_grad.shape[1]))

    def kernel(*refs):
        influence_kernel(rows, scale, *refs)

    operands = [pltpu.with_memory_space_constraint(piece, pltpu.VMEM) for piece in pieces]
    scores = pl.pallas_call(
        kernel,
        out_shape=jax.ShapeDtypeStruct((columns, queries), F32),
        in_specs=[vmem] * len(operands) + [pl.BlockSpec(memory_space=pltpu.HBM)] * 2,
        out_specs=vmem,
        scratch_shapes=[
            pltpu.VMEM(query_act.shape, BF16),
            pltpu.VMEM(query_grad.shape, BF16),
            pltpu.VMEM((tokens, width), BF16),
            pltpu.VMEM((tokens, width), BF16),
            pltpu.VMEM((columns, tokens), BF16),
            pltpu.VMEM((2, width, width), F32),
            pltpu.VMEM((2, width, width), F32),
            pltpu.VMEM((2, width, width), F32),
            pltpu.VMEM((4, width, width), BF16),
            pltpu.SemaphoreType.DMA((2,)),
        ],
        compiler_params=pltpu.CompilerParams(vmem_limit_bytes=40 << 20),
    )(*operands, *(pltpu.with_memory_space_constraint(query, pltpu.HBM) for query in (query_act, query_grad)))
    return scores.T


def local(query_act, query_grad, train_act, train_grad, seq_ids):
    size = lax.axis_size("dp")
    spans, rows, width = train_act.shape
    vmem = pl.BlockSpec(memory_space=pltpu.VMEM)

    def build(*refs):
        payload_kernel(rows, *refs)

    payload = pl.pallas_call(
        build,
        out_shape=pltpu.VMEM((spans, 2 * rows + 8, width), BF16),
        in_specs=[vmem] * 3,
        out_specs=vmem,
    )(train_act, train_grad, seq_ids)
    pieces = gather_spans(payload, size)
    return score_call(pieces, query_act, query_grad, rows)


def solution(mesh):
    in_specs = (
        P(("grp", "dp"), None),
        P(("grp", "dp"), None),
        P(("grp", "dp"), None, None),
        P(("grp", "dp"), None, None),
        P(("grp", "dp"), None),
    )
    out_specs = P(("grp", "dp"), None)
    return jax.shard_map(local, mesh=mesh, in_specs=in_specs, out_specs=out_specs, check_vma=False)
```

profile of v0, /device:TPU:5, one launch (start us, length us, event | category | flops | bytes accessed | tf_op | source)
XLA Modules:
  0.0 33.3 jit_solution(5529482552143726736)
XLA Ops:
  0.0 0.9 %shard_map.55.refs_0_ = bf16[1,136,256]{2,1,0:T(8,128)(2,1)S(1)} custom-call(bf16[1,64,256]{2,1,0:T(8,128)(2,1)} %refs_0_.1, bf16[1,64,256]{2,1,0:T(8,128)(2,1)} %refs_1_.1, s32[1,64]{1,0:T(1,128)} %refs_2_.1), custom_call_target="tpu_custom_call" | custom-call | tf_op jit(solution)/shard_map/pallas_call | solution.py:256
  0.9 2.3 %collective-permute-start.2 = (bf16[1,136,256]{2,1,0:T(8,128)(2,1)S(1)}, bf16[1,136,256]{2,1,0:T(8,128)(2,1)S(1)}, u32[]{:S(2)}, u32[]{:S(2)}) collective-permute-start(bf16[1,136,256]{2,1,0:T(8,128)(2,1)S(1)} %shard_map.55.refs_0_), channel_id=1, source_target_pairs={{0,8},{1,9},{2,10},{3,11},{4,12},{5,13},{6,14},{7,15},{8,0},{9,1},... | collective-permute-start | bytes 208904 | tf_op jit(solution)/shard_map/ppermute | solution.py:200
  3.2 1.0 %collective-permute-start.14 = (bf16[1,136,256]{2,1,0:T(8,128)(2,1)S(1)}, bf16[1,136,256]{2,1,0:T(8,128)(2,1)S(1)}, u32[]{:S(2)}, u32[]{:S(2)}) collective-permute-start(bf16[1,136,256]{2,1,0:T(8,128)(2,1)S(1)} %shard_map.55.refs_0_), channel_id=1, source_target_pairs={{0,1},{1,0},{2,3},{3,2},{4,5},{5,4},{6,7},{7,6},{8,9},{9,8},{10,11... | collective-permute-start | bytes 208904 | tf_op jit(solution)/shard_map/ppermute | solution.py:200
  4.1 1.3 %collective-permute-start.1 = (bf16[1,136,256]{2,1,0:T(8,128)(2,1)S(1)}, bf16[1,136,256]{2,1,0:T(8,128)(2,1)S(1)}, u32[]{:S(2)}, u32[]{:S(2)}) collective-permute-start(bf16[1,136,256]{2,1,0:T(8,128)(2,1)S(1)} %shard_map.55.refs_0_), channel_id=1, source_target_pairs={{0,4},{1,5},{2,6},{3,7},{4,0},{5,1},{6,2},{7,3},{8,12},{9,13},{10,... | collective-permute-start | bytes 208904 | tf_op jit(solution)/shard_map/ppermute | solution.py:200
  5.4 1.2 %collective-permute-start = (bf16[1,136,256]{2,1,0:T(8,128)(2,1)S(1)}, bf16[1,136,256]{2,1,0:T(8,128)(2,1)S(1)}, u32[]{:S(2)}, u32[]{:S(2)}) collective-permute-start(bf16[1,136,256]{2,1,0:T(8,128)(2,1)S(1)} %shard_map.55.refs_0_), channel_id=1, source_target_pairs={{0,2},{1,3},{2,0},{3,1},{4,6},{5,7},{6,4},{7,5},{8,10},{9,11},{10,... | collective-permute-start | bytes 208904 | tf_op jit(solution)/shard_map/ppermute | solution.py:200
  6.6 1.1 %collective-permute-start.13 = (bf16[1,136,256]{2,1,0:T(8,128)(2,1)S(1)}, bf16[1,136,256]{2,1,0:T(8,128)(2,1)S(1)}, u32[]{:S(2)}, u32[]{:S(2)}) collective-permute-start(bf16[1,136,256]{2,1,0:T(8,128)(2,1)S(1)} %collective-permute-done.2.refs_3_), channel_id=1, source_target_pairs={{0,1},{1,0},{2,3},{3,2},{4,5},{5,4},{6,7},{7,6},{8,9},{9,8},{10,11... | collective-permute-start | bytes 208904 | tf_op jit(solution)/shard_map/ppermute | solution.py:200
  7.7 2.0 %collective-permute-start.6 = (bf16[1,136,256]{2,1,0:T(8,128)(2,1)S(1)}, bf16[1,136,256]{2,1,0:T(8,128)(2,1)S(1)}, u32[]{:S(2)}, u32[]{:S(2)}) collective-permute-start(bf16[1,136,256]{2,1,0:T(8,128)(2,1)S(1)} %collective-permute-done.2.refs_3_), channel_id=1, source_target_pairs={{0,6},{1,7},{2,4},{3,5},{4,2},{5,3},{6,0},{7,1},{8,14},{9,15},{10,... | collective-permute-start | bytes 208904 | tf_op jit(solution)/shard_map/ppermute | solution.py:200
  9.7 0.3 collective-permute-start.4
  10.0 0.4 %collective-permute-start.3 = (bf16[1,136,256]{2,1,0:T(8,128)(2,1)S(1)}, bf16[1,136,256]{2,1,0:T(8,128)(2,1)S(1)}, u32[]{:S(2)}, u32[]{:S(2)}) collective-permute-start(bf16[1,136,256]{2,1,0:T(8,128)(2,1)S(1)} %collective-permute-done.2.refs_3_), channel_id=1, source_target_pairs={{0,4},{1,5},{2,6},{3,7},{4,0},{5,1},{6,2},{7,3},{8,12},{9,13},{10,... | collective-permute-start | bytes 208904 | tf_op jit(solution)/shard_map/ppermute | solution.py:200
  10.4 0.0 collective-permute-done.refs_1_
  10.4 0.8 %collective-permute-start.12 = (bf16[1,136,256]{2,1,0:T(8,128)(2,1)S(1)}, bf16[1,136,256]{2,1,0:T(8,128)(2,1)S(1)}, u32[]{:S(2)}, u32[]{:S(2)}) collective-permute-start(bf16[1,136,256]{2,1,0:T(8,128)(2,1)S(1)} %collective-permute-done.1.refs_2_), channel_id=1, source_target_pairs={{0,1},{1,0},{2,3},{3,2},{4,5},{5,4},{6,7},{7,6},{8,9},{9,8},{10,11... | collective-permute-start | bytes 208904 | tf_op jit(solution)/shard_map/ppermute | solution.py:200
  11.2 0.0 collective-permute-done.13.refs_14_
  11.2 1.2 %collective-permute-start.5 = (bf16[1,136,256]{2,1,0:T(8,128)(2,1)S(1)}, bf16[1,136,256]{2,1,0:T(8,128)(2,1)S(1)}, u32[]{:S(2)}, u32[]{:S(2)}) collective-permute-start(bf16[1,136,256]{2,1,0:T(8,128)(2,1)S(1)} %collective-permute-done.1.refs_2_), channel_id=1, source_target_pairs={{0,2},{1,3},{2,0},{3,1},{4,6},{5,7},{6,4},{7,5},{8,10},{9,11},{10,... | collective-permute-start | bytes 208904 | tf_op jit(solution)/shard_map/ppermute | solution.py:200
  12.4 0.0 collective-permute-done.6.refs_7_
  12.4 0.8 %collective-permute-start.11 = (bf16[1,136,256]{2,1,0:T(8,128)(2,1)S(1)}, bf16[1,136,256]{2,1,0:T(8,128)(2,1)S(1)}, u32[]{:S(2)}, u32[]{:S(2)}) collective-permute-start(bf16[1,136,256]{2,1,0:T(8,128)(2,1)S(1)} %collective-permute-done.refs_1_), channel_id=1, source_target_pairs={{0,1},{1,0},{2,3},{3,2},{4,5},{5,4},{6,7},{7,6},{8,9},{9,8},{10,11... | collective-permute-start | bytes 208904 | tf_op jit(solution)/shard_map/ppermute | solution.py:200
  13.3 0.7 %collective-permute-done.4.refs_5_ = bf16[1,136,256]{2,1,0:T(8,128)(2,1)S(1)} collective-permute-done((bf16[1,136,256]{2,1,0:T(8,128)(2,1)S(1)}, bf16[1,136,256]{2,1,0:T(8,128)(2,1)S(1)}, u32[]{:S(2)}, u32[]{:S(2)}) %collective-permute-start.4) | collective-permute-done | bytes 69664 | tf_op jit(solution)/shard_map/ppermute | solution.py:200
  14.0 1.1 %collective-permute-start.7 = (bf16[1,136,256]{2,1,0:T(8,128)(2,1)S(1)}, bf16[1,136,256]{2,1,0:T(8,128)(2,1)S(1)}, u32[]{:S(2)}, u32[]{:S(2)}) collective-permute-start(bf16[1,136,256]{2,1,0:T(8,128)(2,1)S(1)} %collective-permute-done.6.refs_7_), channel_id=1, source_target_pairs={{0,1},{1,0},{2,3},{3,2},{4,5},{5,4},{6,7},{7,6},{8,9},{9,8},{10,11... | collective-permute-start | bytes 208904 | tf_op jit(solution)/shard_map/ppermute | solution.py:200
  15.0 0.0 collective-permute-start.9
  15.1 0.5 %collective-permute-start.10 = (bf16[1,136,256]{2,1,0:T(8,128)(2,1)S(1)}, bf16[1,136,256]{2,1,0:T(8,128)(2,1)S(1)}, u32[]{:S(2)}, u32[]{:S(2)}) collective-permute-start(bf16[1,136,256]{2,1,0:T(8,128)(2,1)S(1)} %collective-permute-done.3.refs_4_), channel_id=1, source_target_pairs={{0,1},{1,0},{2,3},{3,2},{4,5},{5,4},{6,7},{7,6},{8,9},{9,8},{10,11... | collective-permute-start | bytes 208904 | tf_op jit(solution)/shard_map/ppermute | solution.py:200
  15.6 0.6 %collective-permute-start.8 = (bf16[1,136,256]{2,1,0:T(8,128)(2,1)S(1)}, bf16[1,136,256]{2,1,0:T(8,128)(2,1)S(1)}, u32[]{:S(2)}, u32[]{:S(2)}) collective-permute-start(bf16[1,136,256]{2,1,0:T(8,128)(2,1)S(1)} %collective-permute-done.5.refs_6_), channel_id=1, source_target_pairs={{0,1},{1,0},{2,3},{3,2},{4,5},{5,4},{6,7},{7,6},{8,9},{9,8},{10,11... | collective-permute-start | bytes 208904 | tf_op jit(solution)/shard_map/ppermute | solution.py:200
  16.2 0.1 collective-permute-done.9.refs_10_
  16.3 0.2 collective-permute-done.10.refs_11_
  16.5 0.6 %collective-permute-done.8.refs_9_ = bf16[1,136,256]{2,1,0:T(8,128)(2,1)S(1)} collective-permute-done((bf16[1,136,256]{2,1,0:T(8,128)(2,1)S(1)}, bf16[1,136,256]{2,1,0:T(8,128)(2,1)S(1)}, u32[]{:S(2)}, u32[]{:S(2)}) %collective-permute-start.8) | collective-permute-done | bytes 69664 | tf_op jit(solution)/shard_map/ppermute | solution.py:200
  17.1 16.2 %shard_map.56 = f32[64,1024]{1,0:T(8,128)} custom-call(bf16[1,136,256]{2,1,0:T(8,128)(2,1)S(1)} %shard_map.55.refs_0_, bf16[1,136,256]{2,1,0:T(8,128)(2,1)S(1)} %collective-permute-done.refs_1_, bf16[1,136,256]{2,1,0:T(8,128)(2,1)S(1)} %collective-permute-done.1.refs_2_, bf16[1,136,256]{2,1,0:T(8,128)(2,1)S(1)} %collective-permute-done.2.refs_3_, ...), custom_call_target="tpu_custom_call" | custom-call | tf_op jit(solution)/shard_map/pallas_call | solution.py:226
  (8 shorter events, 0.0 us)
Async XLA Ops:
  0.9 5.8 %collective-permute-start.2 = (bf16[1,136,256]{2,1,0:T(8,128)(2,1)S(1)}, bf16[1,136,256]{2,1,0:T(8,128)(2,1)S(1)}, u32[]{:S(2)}, u32[]{:S(2)}) collective-permute-start(bf16[1,136,256]{2,1,0:T(8,128)(2,1)S(1)} %shard_map.55.refs_0_), channel_id=1, source_target_pairs={{0,8},{1,9},{2,10},{3,11},{4,12},{5,13},{6,14},{7,15},{8,0},{9,1},... | collective-permute-start | bytes 208904 | tf_op jit(solution)/shard_map/ppermute | solution.py:200
  3.2 6.5 %collective-permute-start.14 = (bf16[1,136,256]{2,1,0:T(8,128)(2,1)S(1)}, bf16[1,136,256]{2,1,0:T(8,128)(2,1)S(1)}, u32[]{:S(2)}, u32[]{:S(2)}) collective-permute-start(bf16[1,136,256]{2,1,0:T(8,128)(2,1)S(1)} %shard_map.55.refs_0_), channel_id=1, source_target_pairs={{0,1},{1,0},{2,3},{3,2},{4,5},{5,4},{6,7},{7,6},{8,9},{9,8},{10,11... | collective-permute-start | bytes 208904 | tf_op jit(solution)/shard_map/ppermute | solution.py:200
  4.1 5.8 %collective-permute-start.1 = (bf16[1,136,256]{2,1,0:T(8,128)(2,1)S(1)}, bf16[1,136,256]{2,1,0:T(8,128)(2,1)S(1)}, u32[]{:S(2)}, u32[]{:S(2)}) collective-permute-start(bf16[1,136,256]{2,1,0:T(8,128)(2,1)S(1)} %shard_map.55.refs_0_), channel_id=1, source_target_pairs={{0,4},{1,5},{2,6},{3,7},{4,0},{5,1},{6,2},{7,3},{8,12},{9,13},{10,... | collective-permute-start | bytes 208904 | tf_op jit(solution)/shard_map/ppermute | solution.py:200
  5.4 5.0 %collective-permute-start = (bf16[1,136,256]{2,1,0:T(8,128)(2,1)S(1)}, bf16[1,136,256]{2,1,0:T(8,128)(2,1)S(1)}, u32[]{:S(2)}, u32[]{:S(2)}) collective-permute-start(bf16[1,136,256]{2,1,0:T(8,128)(2,1)S(1)} %shard_map.55.refs_0_), channel_id=1, source_target_pairs={{0,2},{1,3},{2,0},{3,1},{4,6},{5,7},{6,4},{7,5},{8,10},{9,11},{10,... | collective-permute-start | bytes 208904 | tf_op jit(solution)/shard_map/ppermute | solution.py:200
  6.6 4.6 %collective-permute-start.13 = (bf16[1,136,256]{2,1,0:T(8,128)(2,1)S(1)}, bf16[1,136,256]{2,1,0:T(8,128)(2,1)S(1)}, u32[]{:S(2)}, u32[]{:S(2)}) collective-permute-start(bf16[1,136,256]{2,1,0:T(8,128)(2,1)S(1)} %collective-permute-done.2.refs_3_), channel_id=1, source_target_pairs={{0,1},{1,0},{2,3},{3,2},{4,5},{5,4},{6,7},{7,6},{8,9},{9,8},{10,11... | collective-permute-start | bytes 208904 | tf_op jit(solution)/shard_map/ppermute | solution.py:200
  7.7 4.7 %collective-permute-start.6 = (bf16[1,136,256]{2,1,0:T(8,128)(2,1)S(1)}, bf16[1,136,256]{2,1,0:T(8,128)(2,1)S(1)}, u32[]{:S(2)}, u32[]{:S(2)}) collective-permute-start(bf16[1,136,256]{2,1,0:T(8,128)(2,1)S(1)} %collective-permute-done.2.refs_3_), channel_id=1, source_target_pairs={{0,6},{1,7},{2,4},{3,5},{4,2},{5,3},{6,0},{7,1},{8,14},{9,15},{10,... | collective-permute-start | bytes 208904 | tf_op jit(solution)/shard_map/ppermute | solution.py:200
  9.7 4.3 %collective-permute-start.4 = (bf16[1,136,256]{2,1,0:T(8,128)(2,1)S(1)}, bf16[1,136,256]{2,1,0:T(8,128)(2,1)S(1)}, u32[]{:S(2)}, u32[]{:S(2)}) collective-permute-start(bf16[1,136,256]{2,1,0:T(8,128)(2,1)S(1)} %collective-permute-done.2.refs_3_), channel_id=1, source_target_pairs={{0,2},{1,3},{2,0},{3,1},{4,6},{5,7},{6,4},{7,5},{8,10},{9,11},{10,... | collective-permute-start | bytes 208904 | tf_op jit(solution)/shard_map/ppermute | solution.py:200
  10.0 5.1 %collective-permute-start.3 = (bf16[1,136,256]{2,1,0:T(8,128)(2,1)S(1)}, bf16[1,136,256]{2,1,0:T(8,128)(2,1)S(1)}, u32[]{:S(2)}, u32[]{:S(2)}) collective-permute-start(bf16[1,136,256]{2,1,0:T(8,128)(2,1)S(1)} %collective-permute-done.2.refs_3_), channel_id=1, source_target_pairs={{0,4},{1,5},{2,6},{3,7},{4,0},{5,1},{6,2},{7,3},{8,12},{9,13},{10,... | collective-permute-start | bytes 208904 | tf_op jit(solution)/shard_map/ppermute | solution.py:200
  10.4 4.7 %collective-permute-start.12 = (bf16[1,136,256]{2,1,0:T(8,128)(2,1)S(1)}, bf16[1,136,256]{2,1,0:T(8,128)(2,1)S(1)}, u32[]{:S(2)}, u32[]{:S(2)}) collective-permute-start(bf16[1,136,256]{2,1,0:T(8,128)(2,1)S(1)} %collective-permute-done.1.refs_2_), channel_id=1, source_target_pairs={{0,1},{1,0},{2,3},{3,2},{4,5},{5,4},{6,7},{7,6},{8,9},{9,8},{10,11... | collective-permute-start | bytes 208904 | tf_op jit(solution)/shard_map/ppermute | solution.py:200
  11.2 4.3 %collective-permute-start.5 = (bf16[1,136,256]{2,1,0:T(8,128)(2,1)S(1)}, bf16[1,136,256]{2,1,0:T(8,128)(2,1)S(1)}, u32[]{:S(2)}, u32[]{:S(2)}) collective-permute-start(bf16[1,136,256]{2,1,0:T(8,128)(2,1)S(1)} %collective-permute-done.1.refs_2_), channel_id=1, source_target_pairs={{0,2},{1,3},{2,0},{3,1},{4,6},{5,7},{6,4},{7,5},{8,10},{9,11},{10,... | collective-permute-start | bytes 208904 | tf_op jit(solution)/shard_map/ppermute | solution.py:200
  12.4 3.8 %collective-permute-start.11 = (bf16[1,136,256]{2,1,0:T(8,128)(2,1)S(1)}, bf16[1,136,256]{2,1,0:T(8,128)(2,1)S(1)}, u32[]{:S(2)}, u32[]{:S(2)}) collective-permute-start(bf16[1,136,256]{2,1,0:T(8,128)(2,1)S(1)} %collective-permute-done.refs_1_), channel_id=1, source_target_pairs={{0,1},{1,0},{2,3},{3,2},{4,5},{5,4},{6,7},{7,6},{8,9},{9,8},{10,11... | collective-permute-start | bytes 208904 | tf_op jit(solution)/shard_map/ppermute | solution.py:200
  14.0 2.2 %collective-permute-start.7 = (bf16[1,136,256]{2,1,0:T(8,128)(2,1)S(1)}, bf16[1,136,256]{2,1,0:T(8,128)(2,1)S(1)}, u32[]{:S(2)}, u32[]{:S(2)}) collective-permute-start(bf16[1,136,256]{2,1,0:T(8,128)(2,1)S(1)} %collective-permute-done.6.refs_7_), channel_id=1, source_target_pairs={{0,1},{1,0},{2,3},{3,2},{4,5},{5,4},{6,7},{7,6},{8,9},{9,8},{10,11... | collective-permute-start | bytes 208904 | tf_op jit(solution)/shard_map/ppermute | solution.py:200
  15.0 1.3 %collective-permute-start.9 = (bf16[1,136,256]{2,1,0:T(8,128)(2,1)S(1)}, bf16[1,136,256]{2,1,0:T(8,128)(2,1)S(1)}, u32[]{:S(2)}, u32[]{:S(2)}) collective-permute-start(bf16[1,136,256]{2,1,0:T(8,128)(2,1)S(1)} %collective-permute-done.4.refs_5_), channel_id=1, source_target_pairs={{0,1},{1,0},{2,3},{3,2},{4,5},{5,4},{6,7},{7,6},{8,9},{9,8},{10,11... | collective-permute-start | bytes 208904 | tf_op jit(solution)/shard_map/ppermute | solution.py:200
  15.1 1.4 %collective-permute-start.10 = (bf16[1,136,256]{2,1,0:T(8,128)(2,1)S(1)}, bf16[1,136,256]{2,1,0:T(8,128)(2,1)S(1)}, u32[]{:S(2)}, u32[]{:S(2)}) collective-permute-start(bf16[1,136,256]{2,1,0:T(8,128)(2,1)S(1)} %collective-permute-done.3.refs_4_), channel_id=1, source_target_pairs={{0,1},{1,0},{2,3},{3,2},{4,5},{5,4},{6,7},{7,6},{8,9},{9,8},{10,11... | collective-permute-start | bytes 208904 | tf_op jit(solution)/shard_map/ppermute | solution.py:200
  15.6 1.5 %collective-permute-start.8 = (bf16[1,136,256]{2,1,0:T(8,128)(2,1)S(1)}, bf16[1,136,256]{2,1,0:T(8,128)(2,1)S(1)}, u32[]{:S(2)}, u32[]{:S(2)}) collective-permute-start(bf16[1,136,256]{2,1,0:T(8,128)(2,1)S(1)} %collective-permute-done.5.refs_6_), channel_id=1, source_target_pairs={{0,1},{1,0},{2,3},{3,2},{4,5},{5,4},{6,7},{7,6},{8,9},{9,8},{10,11... | collective-permute-start | bytes 208904 | tf_op jit(solution)/shard_map/ppermute | solution.py:200
where the time goes:
time: 33.8 us; the launch traced here: 33.3 us
  Pallas kernels  17 us (50%)
  starting transfers between devices  14.6 us (43%)
  waiting for transfers between devices  1.65 us (5%)
    pallas_call x1, Pallas kernels, score_call(): pl.pallas_call(kernel, out_shape=jax.ShapeDtypeStruct((columns, queries),...  16.2 us
    ppermute x15, starting transfers between devices, exchange(): lax.ppermute(piece, 'dp', [(device, device ^ bits) for device in range(si...  14.6 us
    ppermute x15, waiting for transfers between devices, exchange(): lax.ppermute(piece, 'dp', [(device, device ^ bits) for device in range(si...  1.65 us
    pallas_call x1, Pallas kernels, local(): pl.pallas_call(build, out_shape=pltpu.VMEM((spans, 2 * rows + 8, width),...  0.85 us
  transfers between devices with their start and end apart: 15, of which 4 were waited for; matrix products, arithmetic and copies ran while one was open for 0% of the time, Pallas kernels for 0%

commit v1 on v0

--- a/solution.py
+++ b/solution.py
@@ -128,8 +128,11 @@
         both = [
             (factor * (2.0 * x - dot3(split2(x), parts)), t) for (x, _), parts, t in zip(both, tparts, after)
         ]
-    for which in range(2):
-        xmat[which] = both[which][0]
+    for which, x in enumerate(corrected(matrices, [x for x, _ in both], eye)):
+        inverse[2 * which], inverse[2 * which + 1] = split2(x)
+
+    for load in loads:
+        load.wait()
 
     @pl.when(steps > FAST_STEPS)
     def _():
@@ -156,12 +159,10 @@
 
         for which, x in enumerate(corrected([mat[0], mat[1]], [xmat[0], xmat[1]], eye)):
             xmat[which] = x
-
-    for which, x in enumerate(corrected(matrices, [xmat[0], xmat[1]], eye)):
-        inverse[2 * which], inverse[2 * which + 1] = split2(x)
-
-    for load in loads:
-        load.wait()
+        for which, x in enumerate(corrected([mat[0], mat[1]], [xmat[0], xmat[1]], eye)):
+            inverse[2 * which], inverse[2 * which + 1] = split2(x)
+
+
     block, chunk = min(1024, query_act.shape[0]), min(1024, tokens)
 
     def scores(i, carry):
@@ -191,8 +192,8 @@
 
 
 ROUTE_16 = (
-    ((0, 2), (0, 4), (0, 8), (3, 4), (3, 2), (2, 2), (3, 6))
-    + ((7, 1), (6, 1), (5, 1), (4, 1), (1, 1), (2, 1), (3, 1), (0, 1))
+    ((0, 6), (0, 2), (0, 4), (0, 8), (4, 2), (4, 4), (4, 6))
+    + ((7, 1), (1, 1), (5, 1), (6, 1), (2, 1), (3, 1), (4, 1), (0, 1))
 )
 
 

time: 33.8 us -> 25.3 us (0.75)
  the two profiles are of different devices: /device:TPU:5 before, /device:TPU:0 now
where the time goes in v1:
time: 25.3 us; the launch traced here: 25.1 us
  starting transfers between devices  14.4 us (57%)
  Pallas kernels  8.31 us (33%)
  waiting for transfers between devices  2.35 us (9%)
    ppermute x15, starting transfers between devices, exchange(): lax.ppermute(piece, 'dp', [(device, device ^ bits) for device in range(si...  14.4 us
    pallas_call x1, Pallas kernels, score_call(): pl.pallas_call(kernel, out_shape=jax.ShapeDtypeStruct((columns, queries),...  7.46 us
    ppermute x15, waiting for transfers between devices, exchange(): lax.ppermute(piece, 'dp', [(device, device ^ bits) for device in range(si...  2.35 us
    pallas_call x1, Pallas kernels, local(): pl.pallas_call(build, out_shape=pltpu.VMEM((spans, 2 * rows + 8, width),...  0.85 us
  transfers between devices with their start and end apart: 15, of which 6 were waited for; matrix products, arithmetic and copies ran while one was open for 0% of the time, Pallas kernels for 0%

profile of v1, /device:TPU:0, one launch (start us, length us, event | category | flops | bytes accessed | tf_op | source)
XLA Modules:
  0.0 25.1 jit_solution(12776979008261695706)
XLA Ops:
  0.0 0.9 %shard_map.55.refs_0_ = bf16[1,136,256]{2,1,0:T(8,128)(2,1)S(1)} custom-call(bf16[1,64,256]{2,1,0:T(8,128)(2,1)} %refs_0_.1, bf16[1,64,256]{2,1,0:T(8,128)(2,1)} %refs_1_.1, s32[1,64]{1,0:T(1,128)} %refs_2_.1), custom_call_target="tpu_custom_call" | custom-call | tf_op jit(solution)/shard_map/pallas_call | solution.py:257
  0.9 4.0 %collective-permute-start.3 = (bf16[1,136,256]{2,1,0:T(8,128)(2,1)S(1)}, bf16[1,136,256]{2,1,0:T(8,128)(2,1)S(1)}, u32[]{:S(2)}, u32[]{:S(2)}) collective-permute-start(bf16[1,136,256]{2,1,0:T(8,128)(2,1)S(1)} %shard_map.55.refs_0_), channel_id=1, source_target_pairs={{0,8},{1,9},{2,10},{3,11},{4,12},{5,13},{6,14},{7,15},{8,0},{9,1},... | collective-permute-start | bytes 208904 | tf_op jit(solution)/shard_map/ppermute | solution.py:201
  4.9 0.0 collective-permute-start.14
  4.9 1.6 %collective-permute-start.2 = (bf16[1,136,256]{2,1,0:T(8,128)(2,1)S(1)}, bf16[1,136,256]{2,1,0:T(8,128)(2,1)S(1)}, u32[]{:S(2)}, u32[]{:S(2)}) collective-permute-start(bf16[1,136,256]{2,1,0:T(8,128)(2,1)S(1)} %shard_map.55.refs_0_), channel_id=1, source_target_pairs={{0,4},{1,5},{2,6},{3,7},{4,0},{5,1},{6,2},{7,3},{8,12},{9,13},{10,... | collective-permute-start | bytes 208904 | tf_op jit(solution)/shard_map/ppermute | solution.py:201
  6.5 1.5 %collective-permute-start.1 = (bf16[1,136,256]{2,1,0:T(8,128)(2,1)S(1)}, bf16[1,136,256]{2,1,0:T(8,128)(2,1)S(1)}, u32[]{:S(2)}, u32[]{:S(2)}) collective-permute-start(bf16[1,136,256]{2,1,0:T(8,128)(2,1)S(1)} %shard_map.55.refs_0_), channel_id=1, source_target_pairs={{0,2},{1,3},{2,0},{3,1},{4,6},{5,7},{6,4},{7,5},{8,10},{9,11},{10,... | collective-permute-start | bytes 208904 | tf_op jit(solution)/shard_map/ppermute | solution.py:201
  8.0 0.4 %collective-permute-start = (bf16[1,136,256]{2,1,0:T(8,128)(2,1)S(1)}, bf16[1,136,256]{2,1,0:T(8,128)(2,1)S(1)}, u32[]{:S(2)}, u32[]{:S(2)}) collective-permute-start(bf16[1,136,256]{2,1,0:T(8,128)(2,1)S(1)} %shard_map.55.refs_0_), channel_id=1, source_target_pairs={{0,6},{1,7},{2,4},{3,5},{4,2},{5,3},{6,0},{7,1},{8,14},{9,15},{10,... | collective-permute-start | bytes 208904 | tf_op jit(solution)/shard_map/ppermute | solution.py:201
  8.4 0.0 collective-permute-done.14.refs_15_
  8.4 2.6 %collective-permute-start.6 = (bf16[1,136,256]{2,1,0:T(8,128)(2,1)S(1)}, bf16[1,136,256]{2,1,0:T(8,128)(2,1)S(1)}, u32[]{:S(2)}, u32[]{:S(2)}) collective-permute-start(bf16[1,136,256]{2,1,0:T(8,128)(2,1)S(1)} %collective-permute-done.3.refs_4_), channel_id=1, source_target_pairs={{0,6},{1,7},{2,4},{3,5},{4,2},{5,3},{6,0},{7,1},{8,14},{9,15},{10,... | collective-permute-start | bytes 208904 | tf_op jit(solution)/shard_map/ppermute | solution.py:201
  11.0 0.5 %collective-permute-start.5 = (bf16[1,136,256]{2,1,0:T(8,128)(2,1)S(1)}, bf16[1,136,256]{2,1,0:T(8,128)(2,1)S(1)}, u32[]{:S(2)}, u32[]{:S(2)}) collective-permute-start(bf16[1,136,256]{2,1,0:T(8,128)(2,1)S(1)} %collective-permute-done.3.refs_4_), channel_id=1, source_target_pairs={{0,4},{1,5},{2,6},{3,7},{4,0},{5,1},{6,2},{7,3},{8,12},{9,13},{10,... | collective-permute-start | bytes 208904 | tf_op jit(solution)/shard_map/ppermute | solution.py:201
  11.5 2.3 %collective-permute-start.4 = (bf16[1,136,256]{2,1,0:T(8,128)(2,1)S(1)}, bf16[1,136,256]{2,1,0:T(8,128)(2,1)S(1)}, u32[]{:S(2)}, u32[]{:S(2)}) collective-permute-start(bf16[1,136,256]{2,1,0:T(8,128)(2,1)S(1)} %collective-permute-done.3.refs_4_), channel_id=1, source_target_pairs={{0,2},{1,3},{2,0},{3,1},{4,6},{5,7},{6,4},{7,5},{8,10},{9,11},{10,... | collective-permute-start | bytes 208904 | tf_op jit(solution)/shard_map/ppermute | solution.py:201
  13.8 0.1 collective-permute-done.refs_1_
  13.9 0.0 collective-permute-start.12
  13.9 0.5 %collective-permute-start.11 = (bf16[1,136,256]{2,1,0:T(8,128)(2,1)S(1)}, bf16[1,136,256]{2,1,0:T(8,128)(2,1)S(1)}, u32[]{:S(2)}, u32[]{:S(2)}) collective-permute-start(bf16[1,136,256]{2,1,0:T(8,128)(2,1)S(1)} %collective-permute-done.1.refs_2_), channel_id=1, source_target_pairs={{0,1},{1,0},{2,3},{3,2},{4,5},{5,4},{6,7},{7,6},{8,9},{9,8},{10,11... | collective-permute-start | bytes 208904 | tf_op jit(solution)/shard_map/ppermute | solution.py:201
  14.4 1.0 %collective-permute-done.6.refs_7_ = bf16[1,136,256]{2,1,0:T(8,128)(2,1)S(1)} collective-permute-done((bf16[1,136,256]{2,1,0:T(8,128)(2,1)S(1)}, bf16[1,136,256]{2,1,0:T(8,128)(2,1)S(1)}, u32[]{:S(2)}, u32[]{:S(2)}) %collective-permute-start.6) | collective-permute-done | bytes 69664 | tf_op jit(solution)/shard_map/ppermute | solution.py:201
  15.5 0.0 collective-permute-done.5.refs_6_
  15.5 0.5 %collective-permute-start.7 = (bf16[1,136,256]{2,1,0:T(8,128)(2,1)S(1)}, bf16[1,136,256]{2,1,0:T(8,128)(2,1)S(1)}, u32[]{:S(2)}, u32[]{:S(2)}) collective-permute-start(bf16[1,136,256]{2,1,0:T(8,128)(2,1)S(1)} %collective-permute-done.6.refs_7_), channel_id=1, source_target_pairs={{0,1},{1,0},{2,3},{3,2},{4,5},{5,4},{6,7},{7,6},{8,9},{9,8},{10,11... | collective-permute-start | bytes 208904 | tf_op jit(solution)/shard_map/ppermute | solution.py:201
  16.0 0.2 collective-permute-done.4.refs_5_
  16.2 0.0 collective-permute-start.10
  16.2 0.5 %collective-permute-start.9 = (bf16[1,136,256]{2,1,0:T(8,128)(2,1)S(1)}, bf16[1,136,256]{2,1,0:T(8,128)(2,1)S(1)}, u32[]{:S(2)}, u32[]{:S(2)}) collective-permute-start(bf16[1,136,256]{2,1,0:T(8,128)(2,1)S(1)} %collective-permute-done.4.refs_5_), channel_id=1, source_target_pairs={{0,1},{1,0},{2,3},{3,2},{4,5},{5,4},{6,7},{7,6},{8,9},{9,8},{10,11... | collective-permute-start | bytes 208904 | tf_op jit(solution)/shard_map/ppermute | solution.py:201
  16.7 0.0 collective-permute-done.8.refs_9_
  16.7 0.2 collective-permute-done.7.refs_8_
  16.9 0.6 %collective-permute-done.10.refs_11_ = bf16[1,136,256]{2,1,0:T(8,128)(2,1)S(1)} collective-permute-done((bf16[1,136,256]{2,1,0:T(8,128)(2,1)S(1)}, bf16[1,136,256]{2,1,0:T(8,128)(2,1)S(1)}, u32[]{:S(2)}, u32[]{:S(2)}) %collective-permute-start.10) | collective-permute-done | bytes 69664 | tf_op jit(solution)/shard_map/ppermute | solution.py:201
  17.5 0.2 collective-permute-done.9.refs_10_
  17.6 7.5 %shard_map.56 = f32[64,1024]{1,0:T(8,128)} custom-call(bf16[1,136,256]{2,1,0:T(8,128)(2,1)S(1)} %shard_map.55.refs_0_, bf16[1,136,256]{2,1,0:T(8,128)(2,1)S(1)} %collective-permute-done.refs_1_, bf16[1,136,256]{2,1,0:T(8,128)(2,1)S(1)} %collective-permute-done.1.refs_2_, bf16[1,136,256]{2,1,0:T(8,128)(2,1)S(1)} %collective-permute-done.2.refs_3_, ...), custom_call_target="tpu_custom_call" | custom-call | tf_op jit(solution)/shard_map/pallas_call | solution.py:227
  (8 shorter events, 0.0 us)
Async XLA Ops:
  0.9 7.5 %collective-permute-start.3 = (bf16[1,136,256]{2,1,0:T(8,128)(2,1)S(1)}, bf16[1,136,256]{2,1,0:T(8,128)(2,1)S(1)}, u32[]{:S(2)}, u32[]{:S(2)}) collective-permute-start(bf16[1,136,256]{2,1,0:T(8,128)(2,1)S(1)} %shard_map.55.refs_0_), channel_id=1, source_target_pairs={{0,8},{1,9},{2,10},{3,11},{4,12},{5,13},{6,14},{7,15},{8,0},{9,1},... | collective-permute-start | bytes 208904 | tf_op jit(solution)/shard_map/ppermute | solution.py:201
  4.9 3.5 %collective-permute-start.14 = (bf16[1,136,256]{2,1,0:T(8,128)(2,1)S(1)}, bf16[1,136,256]{2,1,0:T(8,128)(2,1)S(1)}, u32[]{:S(2)}, u32[]{:S(2)}) collective-permute-start(bf16[1,136,256]{2,1,0:T(8,128)(2,1)S(1)} %shard_map.55.refs_0_), channel_id=1, source_target_pairs={{0,1},{1,0},{2,3},{3,2},{4,5},{5,4},{6,7},{7,6},{8,9},{9,8},{10,11... | collective-permute-start | bytes 208904 | tf_op jit(solution)/shard_map/ppermute | solution.py:201
  4.9 6.1 %collective-permute-start.2 = (bf16[1,136,256]{2,1,0:T(8,128)(2,1)S(1)}, bf16[1,136,256]{2,1,0:T(8,128)(2,1)S(1)}, u32[]{:S(2)}, u32[]{:S(2)}) collective-permute-start(bf16[1,136,256]{2,1,0:T(8,128)(2,1)S(1)} %shard_map.55.refs_0_), channel_id=1, source_target_pairs={{0,4},{1,5},{2,6},{3,7},{4,0},{5,1},{6,2},{7,3},{8,12},{9,13},{10,... | collective-permute-start | bytes 208904 | tf_op jit(solution)/shard_map/ppermute | solution.py:201
  6.5 5.0 %collective-permute-start.1 = (bf16[1,136,256]{2,1,0:T(8,128)(2,1)S(1)}, bf16[1,136,256]{2,1,0:T(8,128)(2,1)S(1)}, u32[]{:S(2)}, u32[]{:S(2)}) collective-permute-start(bf16[1,136,256]{2,1,0:T(8,128)(2,1)S(1)} %shard_map.55.refs_0_), channel_id=1, source_target_pairs={{0,2},{1,3},{2,0},{3,1},{4,6},{5,7},{6,4},{7,5},{8,10},{9,11},{10,... | collective-permute-start | bytes 208904 | tf_op jit(solution)/shard_map/ppermute | solution.py:201
  8.0 6.0 %collective-permute-start = (bf16[1,136,256]{2,1,0:T(8,128)(2,1)S(1)}, bf16[1,136,256]{2,1,0:T(8,128)(2,1)S(1)}, u32[]{:S(2)}, u32[]{:S(2)}) collective-permute-start(bf16[1,136,256]{2,1,0:T(8,128)(2,1)S(1)} %shard_map.55.refs_0_), channel_id=1, source_target_pairs={{0,6},{1,7},{2,4},{3,5},{4,2},{5,3},{6,0},{7,1},{8,14},{9,15},{10,... | collective-permute-start | bytes 208904 | tf_op jit(solution)/shard_map/ppermute | solution.py:201
  8.4 5.5 %collective-permute-start.13 = (bf16[1,136,256]{2,1,0:T(8,128)(2,1)S(1)}, bf16[1,136,256]{2,1,0:T(8,128)(2,1)S(1)}, u32[]{:S(2)}, u32[]{:S(2)}) collective-permute-start(bf16[1,136,256]{2,1,0:T(8,128)(2,1)S(1)} %collective-permute-done.3.refs_4_), channel_id=1, source_target_pairs={{0,1},{1,0},{2,3},{3,2},{4,5},{5,4},{6,7},{7,6},{8,9},{9,8},{10,11... | collective-permute-start | bytes 208904 | tf_op jit(solution)/shard_map/ppermute | solution.py:201
  8.4 7.1 %collective-permute-start.6 = (bf16[1,136,256]{2,1,0:T(8,128)(2,1)S(1)}, bf16[1,136,256]{2,1,0:T(8,128)(2,1)S(1)}, u32[]{:S(2)}, u32[]{:S(2)}) collective-permute-start(bf16[1,136,256]{2,1,0:T(8,128)(2,1)S(1)} %collective-permute-done.3.refs_4_), channel_id=1, source_target_pairs={{0,6},{1,7},{2,4},{3,5},{4,2},{5,3},{6,0},{7,1},{8,14},{9,15},{10,... | collective-permute-start | bytes 208904 | tf_op jit(solution)/shard_map/ppermute | solution.py:201
  11.0 4.5 %collective-permute-start.5 = (bf16[1,136,256]{2,1,0:T(8,128)(2,1)S(1)}, bf16[1,136,256]{2,1,0:T(8,128)(2,1)S(1)}, u32[]{:S(2)}, u32[]{:S(2)}) collective-permute-start(bf16[1,136,256]{2,1,0:T(8,128)(2,1)S(1)} %collective-permute-done.3.refs_4_), channel_id=1, source_target_pairs={{0,4},{1,5},{2,6},{3,7},{4,0},{5,1},{6,2},{7,3},{8,12},{9,13},{10,... | collective-permute-start | bytes 208904 | tf_op jit(solution)/shard_map/ppermute | solution.py:201
  11.5 4.7 %collective-permute-start.4 = (bf16[1,136,256]{2,1,0:T(8,128)(2,1)S(1)}, bf16[1,136,256]{2,1,0:T(8,128)(2,1)S(1)}, u32[]{:S(2)}, u32[]{:S(2)}) collective-permute-start(bf16[1,136,256]{2,1,0:T(8,128)(2,1)S(1)} %collective-permute-done.3.refs_4_), channel_id=1, source_target_pairs={{0,2},{1,3},{2,0},{3,1},{4,6},{5,7},{6,4},{7,5},{8,10},{9,11},{10,... | collective-permute-start | bytes 208904 | tf_op jit(solution)/shard_map/ppermute | solution.py:201
  13.9 2.3 %collective-permute-start.12 = (bf16[1,136,256]{2,1,0:T(8,128)(2,1)S(1)}, bf16[1,136,256]{2,1,0:T(8,128)(2,1)S(1)}, u32[]{:S(2)}, u32[]{:S(2)}) collective-permute-start(bf16[1,136,256]{2,1,0:T(8,128)(2,1)S(1)} %collective-permute-done.2.refs_3_), channel_id=1, source_target_pairs={{0,1},{1,0},{2,3},{3,2},{4,5},{5,4},{6,7},{7,6},{8,9},{9,8},{10,11... | collective-permute-start | bytes 208904 | tf_op jit(solution)/shard_map/ppermute | solution.py:201
  13.9 2.8 %collective-permute-start.11 = (bf16[1,136,256]{2,1,0:T(8,128)(2,1)S(1)}, bf16[1,136,256]{2,1,0:T(8,128)(2,1)S(1)}, u32[]{:S(2)}, u32[]{:S(2)}) collective-permute-start(bf16[1,136,256]{2,1,0:T(8,128)(2,1)S(1)} %collective-permute-done.1.refs_2_), channel_id=1, source_target_pairs={{0,1},{1,0},{2,3},{3,2},{4,5},{5,4},{6,7},{7,6},{8,9},{9,8},{10,11... | collective-permute-start | bytes 208904 | tf_op jit(solution)/shard_map/ppermute | solution.py:201
  15.5 1.3 %collective-permute-start.8 = (bf16[1,136,256]{2,1,0:T(8,128)(2,1)S(1)}, bf16[1,136,256]{2,1,0:T(8,128)(2,1)S(1)}, u32[]{:S(2)}, u32[]{:S(2)}) collective-permute-start(bf16[1,136,256]{2,1,0:T(8,128)(2,1)S(1)} %collective-permute-done.refs_1_), channel_id=1, source_target_pairs={{0,1},{1,0},{2,3},{3,2},{4,5},{5,4},{6,7},{7,6},{8,9},{9,8},{10,11... | collective-permute-start | bytes 208904 | tf_op jit(solution)/shard_map/ppermute | solution.py:201
  15.5 1.4 %collective-permute-start.7 = (bf16[1,136,256]{2,1,0:T(8,128)(2,1)S(1)}, bf16[1,136,256]{2,1,0:T(8,128)(2,1)S(1)}, u32[]{:S(2)}, u32[]{:S(2)}) collective-permute-start(bf16[1,136,256]{2,1,0:T(8,128)(2,1)S(1)} %collective-permute-done.6.refs_7_), channel_id=1, source_target_pairs={{0,1},{1,0},{2,3},{3,2},{4,5},{5,4},{6,7},{7,6},{8,9},{9,8},{10,11... | collective-permute-start | bytes 208904 | tf_op jit(solution)/shard_map/ppermute | solution.py:201
  16.2 1.3 %collective-permute-start.10 = (bf16[1,136,256]{2,1,0:T(8,128)(2,1)S(1)}, bf16[1,136,256]{2,1,0:T(8,128)(2,1)S(1)}, u32[]{:S(2)}, u32[]{:S(2)}) collective-permute-start(bf16[1,136,256]{2,1,0:T(8,128)(2,1)S(1)} %collective-permute-done.5.refs_6_), channel_id=1, source_target_pairs={{0,1},{1,0},{2,3},{3,2},{4,5},{5,4},{6,7},{7,6},{8,9},{9,8},{10,11... | collective-permute-start | bytes 208904 | tf_op jit(solution)/shard_map/ppermute | solution.py:201
  16.2 1.4 %collective-permute-start.9 = (bf16[1,136,256]{2,1,0:T(8,128)(2,1)S(1)}, bf16[1,136,256]{2,1,0:T(8,128)(2,1)S(1)}, u32[]{:S(2)}, u32[]{:S(2)}) collective-permute-start(bf16[1,136,256]{2,1,0:T(8,128)(2,1)S(1)} %collective-permute-done.4.refs_5_), channel_id=1, source_target_pairs={{0,1},{1,0},{2,3},{3,2},{4,5},{5,4},{6,7},{7,6},{8,9},{9,8},{10,11... | collective-permute-start | bytes 208904 | tf_op jit(solution)/shard_map/ppermute | solution.py:201

commit v2 on v1

--- a/solution.py
+++ b/solution.py
@@ -193,7 +193,7 @@
 
 ROUTE_16 = (
     ((0, 6), (0, 2), (0, 4), (0, 8), (4, 2), (4, 4), (4, 6))
-    + ((7, 1), (1, 1), (5, 1), (6, 1), (2, 1), (3, 1), (4, 1), (0, 1))
+    + ((5, 1), (1, 1), (7, 1), (6, 1), (2, 1), (3, 1), (4, 1), (0, 1))
 )
 
 

time: 25.3 us -> 35 us (1.38)
  Pallas kernels: 8.31 us -> 18.1 us
    pallas_call x1, Pallas kernels: 7.46 us -> 17.2 us  [score_call(): pl.pallas_call(kernel, out_shape=jax.ShapeDtypeStruct((columns, queries),...]
where the time goes in v2:
time: 35 us; the launch traced here: 34.9 us
  Pallas kernels  18.1 us (52%)
  starting transfers between devices  14.4 us (41%)
  waiting for transfers between devices  2.35 us (7%)
    pallas_call x1, Pallas kernels, score_call(): pl.pallas_call(kernel, out_shape=jax.ShapeDtypeStruct((columns, queries),...  17.2 us
    ppermute x15, starting transfers between devices, exchange(): lax.ppermute(piece, 'dp', [(device, device ^ bits) for device in range(si...  14.4 us
    ppermute x15, waiting for transfers between devices, exchange(): lax.ppermute(piece, 'dp', [(device, device ^ bits) for device in range(si...  2.35 us
    pallas_call x1, Pallas kernels, local(): pl.pallas_call(build, out_shape=pltpu.VMEM((spans, 2 * rows + 8, width),...  0.85 us
  transfers between devices with their start and end apart: 15, of which 6 were waited for; matrix products, arithmetic and copies ran while one was open for 0% of the time, Pallas kernels for 0%

profile of v2, /device:TPU:0, one launch (start us, length us, event | category | flops | bytes accessed | tf_op | source)
XLA Modules:
  0.0 34.9 jit_solution(2733473748034538323)
XLA Ops:
  0.0 0.9 %shard_map.55.refs_0_ = bf16[1,136,256]{2,1,0:T(8,128)(2,1)S(1)} custom-call(bf16[1,64,256]{2,1,0:T(8,128)(2,1)} %refs_0_.1, bf16[1,64,256]{2,1,0:T(8,128)(2,1)} %refs_1_.1, s32[1,64]{1,0:T(1,128)} %refs_2_.1), custom_call_target="tpu_custom_call" | custom-call | tf_op jit(solution)/shard_map/pallas_call | solution.py:257
  0.9 4.0 %collective-permute-start.3 = (bf16[1,136,256]{2,1,0:T(8,128)(2,1)S(1)}, bf16[1,136,256]{2,1,0:T(8,128)(2,1)S(1)}, u32[]{:S(2)}, u32[]{:S(2)}) collective-permute-start(bf16[1,136,256]{2,1,0:T(8,128)(2,1)S(1)} %shard_map.55.refs_0_), channel_id=1, source_target_pairs={{0,8},{1,9},{2,10},{3,11},{4,12},{5,13},{6,14},{7,15},{8,0},{9,1},... | collective-permute-start | bytes 208904 | tf_op jit(solution)/shard_map/ppermute | solution.py:201
  4.9 0.0 collective-permute-start.14
  4.9 1.6 %collective-permute-start.2 = (bf16[1,136,256]{2,1,0:T(8,128)(2,1)S(1)}, bf16[1,136,256]{2,1,0:T(8,128)(2,1)S(1)}, u32[]{:S(2)}, u32[]{:S(2)}) collective-permute-start(bf16[1,136,256]{2,1,0:T(8,128)(2,1)S(1)} %shard_map.55.refs_0_), channel_id=1, source_target_pairs={{0,4},{1,5},{2,6},{3,7},{4,0},{5,1},{6,2},{7,3},{8,12},{9,13},{10,... | collective-permute-start | bytes 208904 | tf_op jit(solution)/shard_map/ppermute | solution.py:201
  6.5 1.5 %collective-permute-start.1 = (bf16[1,136,256]{2,1,0:T(8,128)(2,1)S(1)}, bf16[1,136,256]{2,1,0:T(8,128)(2,1)S(1)}, u32[]{:S(2)}, u32[]{:S(2)}) collective-permute-start(bf16[1,136,256]{2,1,0:T(8,128)(2,1)S(1)} %shard_map.55.refs_0_), channel_id=1, source_target_pairs={{0,2},{1,3},{2,0},{3,1},{4,6},{5,7},{6,4},{7,5},{8,10},{9,11},{10,... | collective-permute-start | bytes 208904 | tf_op jit(solution)/shard_map/ppermute | solution.py:201
  8.0 0.4 %collective-permute-start = (bf16[1,136,256]{2,1,0:T(8,128)(2,1)S(1)}, bf16[1,136,256]{2,1,0:T(8,128)(2,1)S(1)}, u32[]{:S(2)}, u32[]{:S(2)}) collective-permute-start(bf16[1,136,256]{2,1,0:T(8,128)(2,1)S(1)} %shard_map.55.refs_0_), channel_id=1, source_target_pairs={{0,6},{1,7},{2,4},{3,5},{4,2},{5,3},{6,0},{7,1},{8,14},{9,15},{10,... | collective-permute-start | bytes 208904 | tf_op jit(solution)/shard_map/ppermute | solution.py:201
  8.4 0.0 collective-permute-done.14.refs_15_
  8.4 2.6 %collective-permute-start.6 = (bf16[1,136,256]{2,1,0:T(8,128)(2,1)S(1)}, bf16[1,136,256]{2,1,0:T(8,128)(2,1)S(1)}, u32[]{:S(2)}, u32[]{:S(2)}) collective-permute-start(bf16[1,136,256]{2,1,0:T(8,128)(2,1)S(1)} %collective-permute-done.3.refs_4_), channel_id=1, source_target_pairs={{0,6},{1,7},{2,4},{3,5},{4,2},{5,3},{6,0},{7,1},{8,14},{9,15},{10,... | collective-permute-start | bytes 208904 | tf_op jit(solution)/shard_map/ppermute | solution.py:201
  11.0 0.5 %collective-permute-start.5 = (bf16[1,136,256]{2,1,0:T(8,128)(2,1)S(1)}, bf16[1,136,256]{2,1,0:T(8,128)(2,1)S(1)}, u32[]{:S(2)}, u32[]{:S(2)}) collective-permute-start(bf16[1,136,256]{2,1,0:T(8,128)(2,1)S(1)} %collective-permute-done.3.refs_4_), channel_id=1, source_target_pairs={{0,4},{1,5},{2,6},{3,7},{4,0},{5,1},{6,2},{7,3},{8,12},{9,13},{10,... | collective-permute-start | bytes 208904 | tf_op jit(solution)/shard_map/ppermute | solution.py:201
  11.5 2.3 %collective-permute-start.4 = (bf16[1,136,256]{2,1,0:T(8,128)(2,1)S(1)}, bf16[1,136,256]{2,1,0:T(8,128)(2,1)S(1)}, u32[]{:S(2)}, u32[]{:S(2)}) collective-permute-start(bf16[1,136,256]{2,1,0:T(8,128)(2,1)S(1)} %collective-permute-done.3.refs_4_), channel_id=1, source_target_pairs={{0,2},{1,3},{2,0},{3,1},{4,6},{5,7},{6,4},{7,5},{8,10},{9,11},{10,... | collective-permute-start | bytes 208904 | tf_op jit(solution)/shard_map/ppermute | solution.py:201
  13.8 0.1 collective-permute-done.refs_1_
  13.9 0.0 collective-permute-start.12
  13.9 0.5 %collective-permute-start.11 = (bf16[1,136,256]{2,1,0:T(8,128)(2,1)S(1)}, bf16[1,136,256]{2,1,0:T(8,128)(2,1)S(1)}, u32[]{:S(2)}, u32[]{:S(2)}) collective-permute-start(bf16[1,136,256]{2,1,0:T(8,128)(2,1)S(1)} %collective-permute-done.1.refs_2_), channel_id=1, source_target_pairs={{0,1},{1,0},{2,3},{3,2},{4,5},{5,4},{6,7},{7,6},{8,9},{9,8},{10,11... | collective-permute-start | bytes 208904 | tf_op jit(solution)/shard_map/ppermute | solution.py:201
  14.4 1.0 %collective-permute-done.6.refs_7_ = bf16[1,136,256]{2,1,0:T(8,128)(2,1)S(1)} collective-permute-done((bf16[1,136,256]{2,1,0:T(8,128)(2,1)S(1)}, bf16[1,136,256]{2,1,0:T(8,128)(2,1)S(1)}, u32[]{:S(2)}, u32[]{:S(2)}) %collective-permute-start.6) | collective-permute-done | bytes 69664 | tf_op jit(solution)/shard_map/ppermute | solution.py:201
  15.5 0.0 collective-permute-done.5.refs_6_
  15.5 0.5 %collective-permute-start.9 = (bf16[1,136,256]{2,1,0:T(8,128)(2,1)S(1)}, bf16[1,136,256]{2,1,0:T(8,128)(2,1)S(1)}, u32[]{:S(2)}, u32[]{:S(2)}) collective-permute-start(bf16[1,136,256]{2,1,0:T(8,128)(2,1)S(1)} %collective-permute-done.6.refs_7_), channel_id=1, source_target_pairs={{0,1},{1,0},{2,3},{3,2},{4,5},{5,4},{6,7},{7,6},{8,9},{9,8},{10,11... | collective-permute-start | bytes 208904 | tf_op jit(solution)/shard_map/ppermute | solution.py:201
  16.0 0.2 collective-permute-done.4.refs_5_
  16.2 0.0 collective-permute-start.10
  16.2 0.5 %collective-permute-start.7 = (bf16[1,136,256]{2,1,0:T(8,128)(2,1)S(1)}, bf16[1,136,256]{2,1,0:T(8,128)(2,1)S(1)}, u32[]{:S(2)}, u32[]{:S(2)}) collective-permute-start(bf16[1,136,256]{2,1,0:T(8,128)(2,1)S(1)} %collective-permute-done.4.refs_5_), channel_id=1, source_target_pairs={{0,1},{1,0},{2,3},{3,2},{4,5},{5,4},{6,7},{7,6},{8,9},{9,8},{10,11... | collective-permute-start | bytes 208904 | tf_op jit(solution)/shard_map/ppermute | solution.py:201
  16.7 0.0 collective-permute-done.8.refs_9_
  16.7 0.2 collective-permute-done.9.refs_10_
  16.9 0.6 %collective-permute-done.10.refs_11_ = bf16[1,136,256]{2,1,0:T(8,128)(2,1)S(1)} collective-permute-done((bf16[1,136,256]{2,1,0:T(8,128)(2,1)S(1)}, bf16[1,136,256]{2,1,0:T(8,128)(2,1)S(1)}, u32[]{:S(2)}, u32[]{:S(2)}) %collective-permute-start.10) | collective-permute-done | bytes 69664 | tf_op jit(solution)/shard_map/ppermute | solution.py:201
  17.5 0.2 collective-permute-done.7.refs_8_
  17.6 17.2 %shard_map.56 = f32[64,1024]{1,0:T(8,128)} custom-call(bf16[1,136,256]{2,1,0:T(8,128)(2,1)S(1)} %shard_map.55.refs_0_, bf16[1,136,256]{2,1,0:T(8,128)(2,1)S(1)} %collective-permute-done.refs_1_, bf16[1,136,256]{2,1,0:T(8,128)(2,1)S(1)} %collective-permute-done.1.refs_2_, bf16[1,136,256]{2,1,0:T(8,128)(2,1)S(1)} %collective-permute-done.2.refs_3_, ...), custom_call_target="tpu_custom_call" | custom-call | tf_op jit(solution)/shard_map/pallas_call | solution.py:227
  (8 shorter events, 0.0 us)
Async XLA Ops:
  0.9 7.5 %collective-permute-start.3 = (bf16[1,136,256]{2,1,0:T(8,128)(2,1)S(1)}, bf16[1,136,256]{2,1,0:T(8,128)(2,1)S(1)}, u32[]{:S(2)}, u32[]{:S(2)}) collective-permute-start(bf16[1,136,256]{2,1,0:T(8,128)(2,1)S(1)} %shard_map.55.refs_0_), channel_id=1, source_target_pairs={{0,8},{1,9},{2,10},{3,11},{4,12},{5,13},{6,14},{7,15},{8,0},{9,1},... | collective-permute-start | bytes 208904 | tf_op jit(solution)/shard_map/ppermute | solution.py:201
  4.9 3.5 %collective-permute-start.14 = (bf16[1,136,256]{2,1,0:T(8,128)(2,1)S(1)}, bf16[1,136,256]{2,1,0:T(8,128)(2,1)S(1)}, u32[]{:S(2)}, u32[]{:S(2)}) collective-permute-start(bf16[1,136,256]{2,1,0:T(8,128)(2,1)S(1)} %shard_map.55.refs_0_), channel_id=1, source_target_pairs={{0,1},{1,0},{2,3},{3,2},{4,5},{5,4},{6,7},{7,6},{8,9},{9,8},{10,11... | collective-permute-start | bytes 208904 | tf_op jit(solution)/shard_map/ppermute | solution.py:201
  4.9 6.1 %collective-permute-start.2 = (bf16[1,136,256]{2,1,0:T(8,128)(2,1)S(1)}, bf16[1,136,256]{2,1,0:T(8,128)(2,1)S(1)}, u32[]{:S(2)}, u32[]{:S(2)}) collective-permute-start(bf16[1,136,256]{2,1,0:T(8,128)(2,1)S(1)} %shard_map.55.refs_0_), channel_id=1, source_target_pairs={{0,4},{1,5},{2,6},{3,7},{4,0},{5,1},{6,2},{7,3},{8,12},{9,13},{10,... | collective-permute-start | bytes 208904 | tf_op jit(solution)/shard_map/ppermute | solution.py:201
  6.5 5.0 %collective-permute-start.1 = (bf16[1,136,256]{2,1,0:T(8,128)(2,1)S(1)}, bf16[1,136,256]{2,1,0:T(8,128)(2,1)S(1)}, u32[]{:S(2)}, u32[]{:S(2)}) collective-permute-start(bf16[1,136,256]{2,1,0:T(8,128)(2,1)S(1)} %shard_map.55.refs_0_), channel_id=1, source_target_pairs={{0,2},{1,3},{2,0},{3,1},{4,6},{5,7},{6,4},{7,5},{8,10},{9,11},{10,... | collective-permute-start | bytes 208904 | tf_op jit(solution)/shard_map/ppermute | solution.py:201
  8.0 6.0 %collective-permute-start = (bf16[1,136,256]{2,1,0:T(8,128)(2,1)S(1)}, bf16[1,136,256]{2,1,0:T(8,128)(2,1)S(1)}, u32[]{:S(2)}, u32[]{:S(2)}) collective-permute-start(bf16[1,136,256]{2,1,0:T(8,128)(2,1)S(1)} %shard_map.55.refs_0_), channel_id=1, source_target_pairs={{0,6},{1,7},{2,4},{3,5},{4,2},{5,3},{6,0},{7,1},{8,14},{9,15},{10,... | collective-permute-start | bytes 208904 | tf_op jit(solution)/shard_map/ppermute | solution.py:201
  8.4 5.5 %collective-permute-start.13 = (bf16[1,136,256]{2,1,0:T(8,128)(2,1)S(1)}, bf16[1,136,256]{2,1,0:T(8,128)(2,1)S(1)}, u32[]{:S(2)}, u32[]{:S(2)}) collective-permute-start(bf16[1,136,256]{2,1,0:T(8,128)(2,1)S(1)} %collective-permute-done.3.refs_4_), channel_id=1, source_target_pairs={{0,1},{1,0},{2,3},{3,2},{4,5},{5,4},{6,7},{7,6},{8,9},{9,8},{10,11... | collective-permute-start | bytes 208904 | tf_op jit(solution)/shard_map/ppermute | solution.py:201
  8.4 7.1 %collective-permute-start.6 = (bf16[1,136,256]{2,1,0:T(8,128)(2,1)S(1)}, bf16[1,136,256]{2,1,0:T(8,128)(2,1)S(1)}, u32[]{:S(2)}, u32[]{:S(2)}) collective-permute-start(bf16[1,136,256]{2,1,0:T(8,128)(2,1)S(1)} %collective-permute-done.3.refs_4_), channel_id=1, source_target_pairs={{0,6},{1,7},{2,4},{3,5},{4,2},{5,3},{6,0},{7,1},{8,14},{9,15},{10,... | collective-permute-start | bytes 208904 | tf_op jit(solution)/shard_map/ppermute | solution.py:201
  11.0 4.5 %collective-permute-start.5 = (bf16[1,136,256]{2,1,0:T(8,128)(2,1)S(1)}, bf16[1,136,256]{2,1,0:T(8,128)(2,1)S(1)}, u32[]{:S(2)}, u32[]{:S(2)}) collective-permute-start(bf16[1,136,256]{2,1,0:T(8,128)(2,1)S(1)} %collective-permute-done.3.refs_4_), channel_id=1, source_target_pairs={{0,4},{1,5},{2,6},{3,7},{4,0},{5,1},{6,2},{7,3},{8,12},{9,13},{10,... | collective-permute-start | bytes 208904 | tf_op jit(solution)/shard_map/ppermute | solution.py:201
  11.5 4.7 %collective-permute-start.4 = (bf16[1,136,256]{2,1,0:T(8,128)(2,1)S(1)}, bf16[1,136,256]{2,1,0:T(8,128)(2,1)S(1)}, u32[]{:S(2)}, u32[]{:S(2)}) collective-permute-start(bf16[1,136,256]{2,1,0:T(8,128)(2,1)S(1)} %collective-permute-done.3.refs_4_), channel_id=1, source_target_pairs={{0,2},{1,3},{2,0},{3,1},{4,6},{5,7},{6,4},{7,5},{8,10},{9,11},{10,... | collective-permute-start | bytes 208904 | tf_op jit(solution)/shard_map/ppermute | solution.py:201
  13.9 2.3 %collective-permute-start.12 = (bf16[1,136,256]{2,1,0:T(8,128)(2,1)S(1)}, bf16[1,136,256]{2,1,0:T(8,128)(2,1)S(1)}, u32[]{:S(2)}, u32[]{:S(2)}) collective-permute-start(bf16[1,136,256]{2,1,0:T(8,128)(2,1)S(1)} %collective-permute-done.2.refs_3_), channel_id=1, source_target_pairs={{0,1},{1,0},{2,3},{3,2},{4,5},{5,4},{6,7},{7,6},{8,9},{9,8},{10,11... | collective-permute-start | bytes 208904 | tf_op jit(solution)/shard_map/ppermute | solution.py:201
  13.9 2.8 %collective-permute-start.11 = (bf16[1,136,256]{2,1,0:T(8,128)(2,1)S(1)}, bf16[1,136,256]{2,1,0:T(8,128)(2,1)S(1)}, u32[]{:S(2)}, u32[]{:S(2)}) collective-permute-start(bf16[1,136,256]{2,1,0:T(8,128)(2,1)S(1)} %collective-permute-done.1.refs_2_), channel_id=1, source_target_pairs={{0,1},{1,0},{2,3},{3,2},{4,5},{5,4},{6,7},{7,6},{8,9},{9,8},{10,11... | collective-permute-start | bytes 208904 | tf_op jit(solution)/shard_map/ppermute | solution.py:201
  15.5 1.3 %collective-permute-start.8 = (bf16[1,136,256]{2,1,0:T(8,128)(2,1)S(1)}, bf16[1,136,256]{2,1,0:T(8,128)(2,1)S(1)}, u32[]{:S(2)}, u32[]{:S(2)}) collective-permute-start(bf16[1,136,256]{2,1,0:T(8,128)(2,1)S(1)} %collective-permute-done.refs_1_), channel_id=1, source_target_pairs={{0,1},{1,0},{2,3},{3,2},{4,5},{5,4},{6,7},{7,6},{8,9},{9,8},{10,11... | collective-permute-start | bytes 208904 | tf_op jit(solution)/shard_map/ppermute | solution.py:201
  15.5 1.4 %collective-permute-start.9 = (bf16[1,136,256]{2,1,0:T(8,128)(2,1)S(1)}, bf16[1,136,256]{2,1,0:T(8,128)(2,1)S(1)}, u32[]{:S(2)}, u32[]{:S(2)}) collective-permute-start(bf16[1,136,256]{2,1,0:T(8,128)(2,1)S(1)} %collective-permute-done.6.refs_7_), channel_id=1, source_target_pairs={{0,1},{1,0},{2,3},{3,2},{4,5},{5,4},{6,7},{7,6},{8,9},{9,8},{10,11... | collective-permute-start | bytes 208904 | tf_op jit(solution)/shard_map/ppermute | solution.py:201
  16.2 1.3 %collective-permute-start.10 = (bf16[1,136,256]{2,1,0:T(8,128)(2,1)S(1)}, bf16[1,136,256]{2,1,0:T(8,128)(2,1)S(1)}, u32[]{:S(2)}, u32[]{:S(2)}) collective-permute-start(bf16[1,136,256]{2,1,0:T(8,128)(2,1)S(1)} %collective-permute-done.5.refs_6_), channel_id=1, source_target_pairs={{0,1},{1,0},{2,3},{3,2},{4,5},{5,4},{6,7},{7,6},{8,9},{9,8},{10,11... | collective-permute-start | bytes 208904 | tf_op jit(solution)/shard_map/ppermute | solution.py:201
  16.2 1.4 %collective-permute-start.7 = (bf16[1,136,256]{2,1,0:T(8,128)(2,1)S(1)}, bf16[1,136,256]{2,1,0:T(8,128)(2,1)S(1)}, u32[]{:S(2)}, u32[]{:S(2)}) collective-permute-start(bf16[1,136,256]{2,1,0:T(8,128)(2,1)S(1)} %collective-permute-done.4.refs_5_), channel_id=1, source_target_pairs={{0,1},{1,0},{2,3},{3,2},{4,5},{5,4},{6,7},{7,6},{8,9},{9,8},{10,11... | collective-permute-start | bytes 208904 | tf_op jit(solution)/shard_map/ppermute | solution.py:201
